TPU v7x, 256 devices: a whole 4x4x8 slice. The times are simulated.
256 devices in a mesh: dp: 8 (over y, core), proto: 32 (over z, x).
Axes of the slice: x: 4, y: 4, z: 8, core: 2. Of those that a mesh axis runs over, the one named last changes fastest.
Arguments:
- teacher_features: bfloat16 [6144, 384], P('dp'), may hold values from -8 to 8
- student_features: bfloat16 [6144, 384], P('dp'), may hold values from -8 to 8
- teacher_weight: bfloat16 [384, 131072], P('dp', 'proto'), may hold values from -1 to 1
- student_weight: bfloat16 [384, 131072], P('dp', 'proto'), may hold values from -1 to 1
Outputs:
- teacher_codes: bfloat16 [6144, 131072], P('dp', 'proto')
- head_loss: float32 [], replicated
- weight_grad: float32 [384, 131072], P('dp', 'proto')
All inputs are finite; a program needn't handle non-finite values.
Results may differ from a plain program's by a relative error of at most 0.003.
Values may be sent and summed in bfloat16 or wider, within the bound.
A program may use at most 128 MiB of HBM per device.

v0:
```python
import jax
import jax.numpy as jnp
from jax import lax
from jax.sharding import PartitionSpec as P

ITERS = 3
teacher_temp = 0.07
student_temp = 0.1
norm_eps = 1e-06


def column_norm(weight_rows):
    return jnp.sqrt(jnp.sum(jnp.square(weight_rows.astype(jnp.float32)), axis=0) + norm_eps)


def body(teacher_features, student_features, teacher_weight, student_weight):
    local_crops = teacher_features.shape[0]
    total_crops = local_crops * lax.axis_size("dp")
    total_protos = teacher_weight.shape[1] * lax.axis_size("proto")
    teacher_full, student_full = (
        lax.all_gather(teacher_weight, "dp", axis=0, tiled=True),
        lax.all_gather(student_weight, "dp", axis=0, tiled=True),
    )
    teacher_norm = column_norm(teacher_full)
    student_norm = column_norm(student_full)
    teacher_logits = (
        jnp.dot(teacher_features, teacher_full, preferred_element_type=jnp.float32) / teacher_norm
    )
    student_logits = (
        jnp.dot(student_features, student_full, preferred_element_type=jnp.float32) / student_norm
    )
    teacher_peak, student_peak = lax.pmax(
        (jnp.max(teacher_logits, axis=1), jnp.max(student_logits, axis=1)), "proto"
    )
    powers = jnp.exp((teacher_logits - teacher_peak[:, None]) / teacher_temp)
    shifted = (student_logits - student_peak[:, None]) / student_temp
    student_local = jnp.sum(jnp.exp(shifted), axis=1)
    crop_scale = jnp.ones((local_crops,), jnp.float32)
    for sweep_index in range(ITERS):
        proto_mass = lax.psum(jnp.dot(crop_scale, powers, precision=lax.Precision.HIGHEST), "dp")
        proto_scale = 1.0 / (total_protos * proto_mass)
        crop_local = jnp.dot(powers, proto_scale, precision=lax.Precision.HIGHEST)
        if sweep_index == 0:
            crop_mass = lax.psum(crop_local, "proto")
        else:
            crop_mass = lax.psum(crop_local, "proto")
        crop_scale = 1.0 / (total_crops * crop_mass)
    student_total = lax.psum(student_local, "proto")
    assign = powers * proto_scale[None, :] * crop_scale[:, None] * total_crops
    teacher_codes = assign.astype(jnp.bfloat16)
    log_prob = shifted - jnp.log(student_total)[:, None]
    loss_local = -jnp.sum(assign * log_prob)
    signal = ((jnp.exp(log_prob) - assign) / student_temp).astype(jnp.bfloat16)
    head_loss = lax.psum(loss_local, ("dp", "proto")) / total_crops
    own_weight = student_weight.astype(jnp.float32) / student_norm
    own_grad = lax.psum_scatter(
        lax.dot_general(
            student_features, signal, (((0,), (0,)), ((), ())), preferred_element_type=jnp.float32
        ),
        "dp",
        scatter_dimension=0,
        tiled=True,
    )
    pressure = lax.psum(jnp.sum(own_grad * own_weight, axis=0), "dp")
    weight_grad = (own_grad - own_weight * pressure[None, :]) / student_norm
    return (teacher_codes, head_loss, weight_grad)


def solution(mesh):
    return jax.shard_map(
        body,
        mesh=mesh,
        in_specs=(P("dp", None), P("dp", None), P("dp", "proto"), P("dp", "proto")),
        out_specs=(P("dp", "proto"), P(), P("dp", "proto")),
        check_vma=False,
    )
```

profile of v0, /device:TPU:32, one launch (start us, length us, event | category | flops | bytes accessed | tf_op | source)
XLA Modules:
  0.0 684.9 jit_solution(6292353373318271310)
XLA Ops:
  8.0 0.7 all-gather.3.cloned.1.call-update
  8.7 34.1 %all-gather.5.cloned.1.call-done = bf16[384,4096]{1,0:T(8,128)(2,1)} async-done(((bf16[48,4096]{1,0:T(8,128)(2,1)}), bf16[384,4096]{1,0:T(8,128)(2,1)}) %all-gather.5.cloned.1.call-update) | async-done | bytes 3145744 | tf_op jit(solution)/shard_map/all_gather | solution.py:22
  42.8 2.6 multiply_reduce_fusion.1
  45.4 29.6 %all-gather.3.cloned.1.call-done = bf16[384,4096]{1,0:T(8,128)(2,1)} async-done(((bf16[48,4096]{1,0:T(8,128)(2,1)}), bf16[384,4096]{1,0:T(8,128)(2,1)}) %all-gather.3.cloned.1.call-update) | async-done | bytes 3145744 | tf_op jit(solution)/shard_map/all_gather | solution.py:21
  75.1 2.6 multiply_reduce_fusion.2
  77.7 8.5 %fusion.9 = (f32[768]{0:T(1024)S(1)}, f32[768,4096]{1,0:T(8,128)}) fusion(f32[4096]{0:T(1024)S(1)} %add_sqrt_fusion, bf16[768,384]{1,0:T(8,128)(2,1)S(1)} %copy-done, bf16[384,4096]{1,0:T(8,128)(2,1)} %all-gather.5.cloned.1.call-done), kind=kOutput, calls=%fused_computation.33 | convolution fusion | flops 2422209792 | bytes 16337920 | tf_op jit(solution)/shard_map/dot_general | solution.py:30
  86.2 6.4 fusion.3
  92.6 70.3 %all-reduce.1 = (f32[768]{0:T(1024)S(1)}, f32[768]{0:T(1024)S(1)}) all-reduce(f32[768]{0:T(1024)S(1)} %get-tuple-element.15, f32[768]{0:T(1024)S(1)} %get-tuple-element.17), channel_id=1, replica_groups=mesh['dp'=8,'proto'=32] {'proto'}, use_global_device_ids=true, to_apply=%region_2.0 | all-reduce | flops 1536 | bytes 12288 | tf_op jit(solution)/shard_map/pmax | solution.py:32
  162.9 10.4 %exponential_reduce_fusion = (f32[768]{0:T(1024)S(1)}, f32[768,4096]{1,0:T(8,128)S(1)}) fusion(f32[768,4096]{1,0:T(8,128)} %get-tuple-element.18, f32[768]{0:T(1024)S(1)} %get-tuple-element.12, f32[768]{0:T(1024)S(1)} %get-tuple-element.11, f32[768,4096]{1,0:T(8,128)} %get-tuple-element.16, f32[4096]{0:T(1024)S(1)} %add_sqrt_fusion.1), kind=kLoop, calls=%fused_computation.2 | loop fusion | flops 18873600 | bytes 37774336 | tf_op jit(solution)/shard_map/reduce_sum | solution.py:37
  173.4 4.5 copy-done.1
  177.8 6.0 fusion.4
  183.8 24.1 %psum.63 = f32[4096]{0:T(1024)S(1)} all-reduce(f32[4096]{0:T(1024)S(1)} %bitcast.30), channel_id=1, replica_groups=mesh['dp'=8,'proto'=32] {'dp'}, use_global_device_ids=true, to_apply=%region_3.0 | all-reduce | flops 4096 | bytes 32768 | tf_op jit(solution)/shard_map/psum | solution.py:40
  207.9 13.3 %convolution_reduce_fusion.2 = f32[768]{0:T(1024)S(1)} fusion(f32[768,4096]{1,0:T(8,128)} %copy-done.1, f32[4096,1]{0,1:T(1,128)S(1)} %bitcast.26), kind=kOutput, calls=%fused_computation.19 | convolution fusion | flops 37748736 | bytes 12602368 | tf_op jit(solution)/shard_map/dot_general | solution.py:42
  221.2 69.6 %psum.64 = f32[768]{0:T(1024)S(1)} all-reduce(f32[768]{0:T(1024)S(1)} %convolution_reduce_fusion.2), channel_id=1, replica_groups=mesh['dp'=8,'proto'=32] {'proto'}, use_global_device_ids=true, to_apply=%region_4.0 | all-reduce | flops 768 | bytes 6144 | tf_op jit(solution)/shard_map/psum | solution.py:44
  290.9 8.5 %fusion.10 = f32[1,4096]{1,0:T(1,128)S(1)} fusion(f32[768,1]{0,1:T(1,128)S(1)} %reshape.24, f32[768,4096]{1,0:T(8,128)} %copy-done.1), kind=kOutput, calls=%fused_computation.34 | convolution fusion | flops 37748736 | bytes 12602368 | tf_op jit(solution)/shard_map/dot_general | solution.py:40
  299.4 23.6 %psum.65 = f32[4096]{0:T(1024)S(1)} all-reduce(f32[4096]{0:T(1024)S(1)} %bitcast.27), channel_id=1, replica_groups=mesh['dp'=8,'proto'=32] {'dp'}, use_global_device_ids=true, to_apply=%region_5.0 | all-reduce | flops 4096 | bytes 32768 | tf_op jit(solution)/shard_map/psum | solution.py:40
  323.0 13.3 %convolution_reduce_fusion.1 = f32[768]{0:T(1024)S(1)} fusion(f32[768,4096]{1,0:T(8,128)} %copy-done.1, f32[4096,1]{0,1:T(1,128)S(1)} %bitcast.28), kind=kOutput, calls=%fused_computation.18 | convolution fusion | flops 37748736 | bytes 12602368 | tf_op jit(solution)/shard_map/dot_general | solution.py:42
  336.3 71.8 %psum.66 = f32[768]{0:T(1024)S(1)} all-reduce(f32[768]{0:T(1024)S(1)} %convolution_reduce_fusion.1), channel_id=1, replica_groups=mesh['dp'=8,'proto'=32] {'proto'}, use_global_device_ids=true, to_apply=%region_6.0 | all-reduce | flops 768 | bytes 6144 | tf_op jit(solution)/shard_map/psum | solution.py:46
  408.1 8.5 %fusion.11 = f32[1,4096]{1,0:T(1,128)S(1)} fusion(f32[768,1]{0,1:T(1,128)S(1)} %reshape.28, f32[768,4096]{1,0:T(8,128)} %copy-done.1), kind=kOutput, calls=%fused_computation.35 | convolution fusion | flops 37748736 | bytes 12602368 | tf_op jit(solution)/shard_map/dot_general | solution.py:40
  416.6 23.6 %psum.67 = f32[4096]{0:T(1024)S(1)} all-reduce(f32[4096]{0:T(1024)S(1)} %bitcast.29), channel_id=1, replica_groups=mesh['dp'=8,'proto'=32] {'dp'}, use_global_device_ids=true, to_apply=%region_7.0 | all-reduce | flops 4096 | bytes 32768 | tf_op jit(solution)/shard_map/psum | solution.py:40
  440.2 13.3 %convolution_reduce_fusion = f32[768]{0:T(1024)S(1)} fusion(f32[768,4096]{1,0:T(8,128)} %copy-done.1, f32[4096,1]{0,1:T(1,128)S(1)} %bitcast.25), kind=kOutput, calls=%fused_computation.17 | convolution fusion | flops 37748736 | bytes 12602368 | tf_op jit(solution)/shard_map/dot_general | solution.py:42
  453.5 70.9 %all-reduce = (f32[768]{0:T(1024)S(1)}, f32[768]{0:T(1024)S(1)}) all-reduce(f32[768]{0:T(1024)S(1)} %convolution_reduce_fusion, f32[768]{0:T(1024)S(1)} %get-tuple-element.19), channel_id=1, replica_groups=mesh['dp'=8,'proto'=32] {'proto'}, use_global_device_ids=true, to_apply=%region_8.0 | all-reduce | flops 1536 | bytes 12288 | tf_op jit(solution)/shard_map/psum | solution.py:46
  524.4 13.1 %fusion.2 = f32[384,4096]{0,1:T(8,128)} fusion(bf16[768,384]{1,0:T(8,128)(2,1)S(1)} %copy-done, f32[768,4096]{1,0:T(8,128)} %get-tuple-element.18, f32[768,4096]{1,0:T(8,128)} %copy-done.1, f32[768]{0:T(1024)S(1)} %log.3, f32[768]{0:T(1024)S(1)} %get-tuple-element.12, f32[768]{0:T(1024)S(1)} %multiply_divide_fusion.3, f32[4096]{0:T(1024)S(1)} %multiply_divide_fusion), kind=kOutput, calls=%fused_computation.12 | convolution fusion | flops 2444230656 | bytes 32072704 | tf_op jit(solution)/shard_map/dot_general | solution.py:57
  537.5 6.5 copy.11
  544.0 14.4 %multiply_reduce_fusion = (f32[]{:T(128)}, bf16[768,4096]{1,0:T(8,128)(2,1)}) fusion(f32[768,4096]{1,0:T(8,128)} %get-tuple-element.18, f32[768,4096]{1,0:T(8,128)} %copy-done.1, f32[768]{0:T(1024)S(1)} %log.3, f32[768]{0:T(1024)S(1)} %get-tuple-element.12, f32[768]{0:T(1024)S(1)} %multiply_divide_fusion.3, f32[4096]{0:T(1024)S(1)} %multiply_divide_fusion), kind=kLoop, calls=%fused_computation.1 | loop fusion | flops 28311552 | bytes 31482884 | tf_op jit(solution)/shard_map/reduce_sum | solution.py:52
  559.1 1.3 copy.9
  560.4 80.6 %psum.70 = f32[]{:T(128)} all-reduce(f32[]{:T(128)S(6)} %neg.3), channel_id=1, replica_groups=mesh['dp'=8,'proto'=32] {'dp','proto'}, use_global_device_ids=true, to_apply=%region_15.0 | all-reduce | flops 1 | bytes 8 | tf_op jit(solution)/shard_map/psum | solution.py:54
  641.7 1.7 copy.12
  643.4 2.3 multiply_reduce_fusion.3
  645.8 23.6 %psum.71 = f32[4096]{0:T(1024)S(1)} all-reduce(f32[4096]{0:T(1024)S(1)} %multiply_reduce_fusion.3), channel_id=1, replica_groups=mesh['dp'=8,'proto'=32] {'dp'}, use_global_device_ids=true, to_apply=%region_18.0 | all-reduce | flops 4096 | bytes 32768 | tf_op jit(solution)/shard_map/psum | solution.py:64
  669.3 4.6 subtract_divide_fusion
  673.9 3.1 copy.10
  (26 shorter events, 0.9 us)
Async XLA Ops:
  7.2 70.5 %copy-start = (bf16[768,384]{1,0:T(8,128)(2,1)S(1)}, bf16[768,384]{1,0:T(8,128)(2,1)}, u32[]{:S(2)}) copy-start(bf16[768,384]{1,0:T(8,128)(2,1)} %param.5) | copy-start | bytes 1769476
  7.2 35.6 %all-gather.5.cloned.1.call-start = ((), (), s32[]{:S(2)}) async-start(), calls=%async_computation.2 | async-start | bytes 3538944 | tf_op jit(solution)/shard_map/all_gather | solution.py:22
  7.9 67.1 %all-gather.3.cloned.1.call-start = ((), (), s32[]{:S(2)}) async-start(), calls=%async_computation.1 | async-start | bytes 3538944 | tf_op jit(solution)/shard_map/all_gather | solution.py:21
  8.7 633.0 %reduce-scatter.4.cloned.1.call-start = ((), (), s32[]{:S(2)}) async-start(), calls=%async_computation.3 | async-start | bytes 7077888
  77.7 8.6 %copy-start.2 = (bf16[384,4096]{1,0:T(8,128)(2,1)S(1)}, bf16[384,4096]{1,0:T(8,128)(2,1)}, u32[]{:S(2)}) copy-start(bf16[384,4096]{1,0:T(8,128)(2,1)} %all-gather.3.cloned.1.call-done) | copy-start | bytes 9437188
  77.7 8.6 %copy-start.4 = (bf16[768,384]{1,0:T(8,128)(2,1)S(1)}, bf16[768,384]{1,0:T(8,128)(2,1)}, u32[]{:S(2)}) copy-start(bf16[768,384]{1,0:T(8,128)(2,1)} %param.4) | copy-start | bytes 1769476
  173.4 4.5 copy-start.1
  544.0 15.1 %copy-start.3 = (bf16[48,4096]{1,0:T(8,128)(2,1)S(1)}, bf16[48,4096]{1,0:T(8,128)(2,1)}, u32[]{:S(2)}) copy-start(bf16[48,4096]{1,0:T(8,128)(2,1)} %param.7) | copy-start | bytes 1179652
Sparse Core Ops, SparseCore 0:
  9.8 32.9 all-gather.4
  44.6 30.3 all-gather.2
  544.2 46.9 reduce-scatter.3
where the time goes:
time: 689 us; the launch traced here: 685 us
  blocking collectives  458 us (66%)
  matrix products  91 us (13%)
  waiting for transfers between devices  65.2 us (9%)
  other arithmetic  37 us (5%)
  local copies, waits for them, and re-layouts  17.1 us (2%)
  between operations  16.6 us (2%)
    psum x3, blocking collectives, body(): crop_mass = lax.psum(crop_local, 'proto')  212 us
    psum x1, blocking collectives, body(): head_loss = lax.psum(loss_local, ('dp', 'proto')) / total_crops  80.6 us
    psum x3, blocking collectives, body(): lax.psum(jnp.dot(crop_scale, powers, precision=lax.Precision.HIGHEST), 'dp')  71.2 us
    pmax x1, blocking collectives, body(): lax.pmax((jnp.max(teacher_logits, axis=1), jnp.max(student_logits, axis=1...  70.3 us
    dot_general x3, matrix products, body(): crop_local = jnp.dot(powers, proto_scale, precision=lax.Precision.HIGHEST)  39.9 us
    all_gather x1, waiting for transfers between devices, body(): lax.all_gather(student_weight, 'dp', axis=0, tiled=True)  34.1 us
    all_gather x1, waiting for transfers between devices, body(): lax.all_gather(teacher_weight, 'dp', axis=0, tiled=True)  29.6 us
    psum x1, blocking collectives, body(): pressure = lax.psum(jnp.sum(own_grad * own_weight, axis=0), 'dp')  23.6 us
  transfers between devices with their start and end apart: 3, of which 2 were waited for; matrix products, arithmetic and copies ran while one was open for 3% of the time, Pallas kernels for 0%

commit v1 on v0

--- a/solution.py
+++ b/solution.py
@@ -7,6 +7,19 @@
 teacher_temp = 0.07
 student_temp = 0.1
 norm_eps = 1e-06
+
+
+def ring_gather(x, axis, dim):
+    ways = lax.axis_size(axis)
+    up = [(d, (d + 1) % ways) for d in range(ways)]
+    down = [(d, (d - 1) % ways) for d in range(ways)]
+    earlier, later = ([x], [x])
+    for _ in range(ways // 2):
+        earlier.append(lax.ppermute(earlier[-1], axis, up))
+    for _ in range((ways - 1) // 2):
+        later.append(lax.ppermute(later[-1], axis, down))
+    line = jnp.concatenate([*earlier[::-1], *later[1:]], axis=dim)
+    return jnp.roll(line, (lax.axis_index(axis) - ways // 2) * x.shape[dim], axis=dim)
 
 
 def column_norm(weight_rows):
@@ -19,7 +32,7 @@
     total_protos = teacher_weight.shape[1] * lax.axis_size("proto")
     teacher_full, student_full = (
         lax.all_gather(teacher_weight, "dp", axis=0, tiled=True),
-        lax.all_gather(student_weight, "dp", axis=0, tiled=True),
+        ring_gather(student_weight, "dp", 0),
     )
     teacher_norm = column_norm(teacher_full)
     student_norm = column_norm(student_full)

time: 689 us -> 674 us (0.978)
  waiting for transfers between devices: 65.2 us -> 40 us
  starting transfers between devices: 0.11 us -> 9.13 us
    all_gather x1 -> x0, waiting for transfers between devices: 34.1 us -> none  [body(): lax.all_gather(student_weight, 'dp', axis=0, tiled=True)]
    ppermute x0 -> x7, waiting for transfers between devices: none -> 24.7 us  [the longest x4 24.6 us: ring_gather(): earlier.append(lax.ppermute(earlier[-1], axis, up))]
    all_gather x1, waiting for transfers between devices: 29.6 us -> 15.2 us  [body(): lax.all_gather(teacher_weight, 'dp', axis=0, tiled=True)]
    ppermute x0 -> x7, starting transfers between devices: none -> 9.05 us  [the longest x3 9.02 us: ring_gather(): later.append(lax.ppermute(later[-1], axis, down))]
    unnamed x14 -> x27, local copies, waits for them, and re-layouts: 17.1 us -> 14.1 us
  transfers between devices with their start and end apart: 3 -> 9, of which waited for: 2 -> 6; matrix products, arithmetic and copies ran while one was open for 3% -> 4% of each run, Pallas kernels for 0% -> 0%
where the time goes in v1:
time: 674 us; the launch traced here: 668 us
  blocking collectives  458 us (68%)
  matrix products  90.9 us (13%)
  waiting for transfers between devices  40 us (6%)
  other arithmetic  39.2 us (6%)
  between operations  17.1 us (3%)
  local copies, waits for them, and re-layouts  14.1 us (2%)
  starting transfers between devices  9.13 us (1%)
    psum x3, blocking collectives, body(): crop_mass = lax.psum(crop_local, 'proto')  212 us
    psum x1, blocking collectives, body(): head_loss = lax.psum(loss_local, ('dp', 'proto')) / total_crops  80.6 us
    psum x3, blocking collectives, body(): lax.psum(jnp.dot(crop_scale, powers, precision=lax.Precision.HIGHEST), 'dp')  70.9 us
    pmax x1, blocking collectives, body(): lax.pmax((jnp.max(teacher_logits, axis=1), jnp.max(student_logits, axis=1...  70.5 us
    dot_general x3, matrix products, body(): crop_local = jnp.dot(powers, proto_scale, precision=lax.Precision.HIGHEST)  39.9 us
    ppermute x4, waiting for transfers between devices, ring_gather(): earlier.append(lax.ppermute(earlier[-1], axis, up))  24.6 us
    psum x1, blocking collectives, body(): pressure = lax.psum(jnp.sum(own_grad * own_weight, axis=0), 'dp')  23.6 us
    dot_general x3, matrix products, body(): jnp.dot(crop_scale, powers, precision=lax.Precision.HIGHEST)  23 us
  transfers between devices with their start and end apart: 9, of which 6 were waited for; matrix products, arithmetic and copies ran while one was open for 4% of the time, Pallas kernels for 0%

profile of v1, /device:TPU:32, one launch (start us, length us, event | category | flops | bytes accessed | tf_op | source)
XLA Modules:
  0.0 668.2 jit_solution(1558070334485101536)
XLA Ops:
  7.3 8.6 %collective-permute-done = bf16[48,4096]{1,0:T(8,128)(2,1)S(1)} collective-permute-done((bf16[48,4096]{1,0:T(8,128)(2,1)}, bf16[48,4096]{1,0:T(8,128)(2,1)S(1)}, u32[]{:S(2)}, u32[]{:S(2)}) %collective-permute-start) | collective-permute-done | bytes 393248 | tf_op jit(solution)/shard_map/ppermute | solution.py:18
  15.9 3.0 collective-permute-start.4
  18.8 5.5 collective-permute-done.1
  24.4 3.0 collective-permute-start.5
  27.5 5.2 collective-permute-done.2
  32.8 3.1 collective-permute-start.6
  35.9 5.2 collective-permute-done.3
  43.8 6.6 fusion.18
  50.4 15.2 %all-gather.2.cloned.1.call-done = bf16[384,4096]{1,0:T(8,128)(2,1)} async-done(((bf16[48,4096]{1,0:T(8,128)(2,1)}), bf16[384,4096]{1,0:T(8,128)(2,1)}) %all-gather.2.cloned.1.call-update) | async-done | bytes 3145744 | tf_op jit(solution)/shard_map/all_gather | solution.py:34
  68.2 8.2 %fusion.10 = (f32[768]{0:T(1024)S(1)}, f32[768,4096]{1,0:T(8,128)}) fusion(f32[4096]{0:T(1024)S(1)} %add_sqrt_fusion.1, bf16[768,384]{1,0:T(8,128)(2,1)S(1)} %copy-done.3, bf16[384,4096]{1,0:T(8,128)(2,1)} %all-gather.2.cloned.1.call-done), kind=kOutput, calls=%fused_computation.17 | convolution fusion | flops 2422209792 | bytes 16337920 | tf_op jit(solution)/shard_map/dot_general | solution.py:40
  76.5 70.5 %all-reduce.1 = (f32[768]{0:T(1024)S(1)}, f32[768]{0:T(1024)S(1)}) all-reduce(f32[768]{0:T(1024)S(1)} %get-tuple-element.15, f32[768]{0:T(1024)S(1)} %get-tuple-element.17), channel_id=1, replica_groups=mesh['dp'=8,'proto'=32] {'proto'}, use_global_device_ids=true, to_apply=%region_2.3 | all-reduce | flops 1536 | bytes 12288 | tf_op jit(solution)/shard_map/pmax | solution.py:45
  147.0 6.1 multiply_exponential_fusion
  153.1 6.0 fusion.12
  159.1 23.5 %psum.63 = f32[4096]{0:T(1024)S(1)} all-reduce(f32[4096]{0:T(1024)S(1)} %bitcast.43), channel_id=1, replica_groups=mesh['dp'=8,'proto'=32] {'dp'}, use_global_device_ids=true, to_apply=%region_3.4 | all-reduce | flops 4096 | bytes 32768 | tf_op jit(solution)/shard_map/psum | solution.py:53
  182.6 13.3 %convolution_reduce_fusion.2 = f32[768]{0:T(1024)S(1)} fusion(f32[768,4096]{1,0:T(8,128)} %copy-done.1, f32[4096,1]{0,1:T(1,128)S(1)} %bitcast.39), kind=kOutput, calls=%fused_computation.24 | convolution fusion | flops 37748736 | bytes 12602368 | tf_op jit(solution)/shard_map/dot_general | solution.py:55
  195.9 69.8 %psum.64 = f32[768]{0:T(1024)S(1)} all-reduce(f32[768]{0:T(1024)S(1)} %convolution_reduce_fusion.2), channel_id=1, replica_groups=mesh['dp'=8,'proto'=32] {'proto'}, use_global_device_ids=true, to_apply=%region_4.5 | all-reduce | flops 768 | bytes 6144 | tf_op jit(solution)/shard_map/psum | solution.py:57
  265.8 8.5 %fusion.19 = f32[1,4096]{1,0:T(1,128)S(1)} fusion(f32[768,1]{0,1:T(1,128)S(1)} %reshape.24, f32[768,4096]{1,0:T(8,128)} %copy-done.1), kind=kOutput, calls=%fused_computation.56 | convolution fusion | flops 37748736 | bytes 12602368 | tf_op jit(solution)/shard_map/dot_general | solution.py:53
  274.3 23.6 %psum.65 = f32[4096]{0:T(1024)S(1)} all-reduce(f32[4096]{0:T(1024)S(1)} %bitcast.40), channel_id=1, replica_groups=mesh['dp'=8,'proto'=32] {'dp'}, use_global_device_ids=true, to_apply=%region_5.6 | all-reduce | flops 4096 | bytes 32768 | tf_op jit(solution)/shard_map/psum | solution.py:53
  297.9 13.3 %convolution_reduce_fusion.1 = f32[768]{0:T(1024)S(1)} fusion(f32[768,4096]{1,0:T(8,128)} %copy-done.1, f32[4096,1]{0,1:T(1,128)S(1)} %bitcast.41), kind=kOutput, calls=%fused_computation.23 | convolution fusion | flops 37748736 | bytes 12602368 | tf_op jit(solution)/shard_map/dot_general | solution.py:55
  311.2 71.6 %psum.66 = f32[768]{0:T(1024)S(1)} all-reduce(f32[768]{0:T(1024)S(1)} %convolution_reduce_fusion.1), channel_id=1, replica_groups=mesh['dp'=8,'proto'=32] {'proto'}, use_global_device_ids=true, to_apply=%region_6.7 | all-reduce | flops 768 | bytes 6144 | tf_op jit(solution)/shard_map/psum | solution.py:59
  382.8 8.5 %fusion.20 = f32[1,4096]{1,0:T(1,128)S(1)} fusion(f32[768,1]{0,1:T(1,128)S(1)} %reshape.28, f32[768,4096]{1,0:T(8,128)} %copy-done.1), kind=kOutput, calls=%fused_computation.57 | convolution fusion | flops 37748736 | bytes 12602368 | tf_op jit(solution)/shard_map/dot_general | solution.py:53
  391.4 23.8 %psum.67 = f32[4096]{0:T(1024)S(1)} all-reduce(f32[4096]{0:T(1024)S(1)} %bitcast.42), channel_id=1, replica_groups=mesh['dp'=8,'proto'=32] {'dp'}, use_global_device_ids=true, to_apply=%region_7.8 | all-reduce | flops 4096 | bytes 32768 | tf_op jit(solution)/shard_map/psum | solution.py:53
  415.2 13.3 %convolution_reduce_fusion = f32[768]{0:T(1024)S(1)} fusion(f32[768,4096]{1,0:T(8,128)} %copy-done.1, f32[4096,1]{0,1:T(1,128)S(1)} %bitcast.38), kind=kOutput, calls=%fused_computation.22 | convolution fusion | flops 37748736 | bytes 12602368 | tf_op jit(solution)/shard_map/dot_general | solution.py:55
  428.5 6.7 %exponential_reduce_fusion = f32[768]{0:T(1024)S(1)} fusion(f32[4096,768]{0,1:T(8,128)} %get-tuple-element.18, f32[768]{0:T(1024)S(1)} %get-tuple-element.12), kind=kLoop, calls=%fused_computation.6 | loop fusion | flops 9436416 | bytes 12589056 | tf_op jit(solution)/shard_map/reduce_sum | solution.py:50
  435.2 70.9 %all-reduce = (f32[768]{0:T(1024)S(1)}, f32[768]{0:T(1024)S(1)}) all-reduce(f32[768]{0:T(1024)S(1)} %convolution_reduce_fusion, f32[768]{0:T(1024)S(1)} %exponential_reduce_fusion), channel_id=1, replica_groups=mesh['dp'=8,'proto'=32] {'proto'}, use_global_device_ids=true, to_apply=%region_8.9 | all-reduce | flops 1536 | bytes 12288 | tf_op jit(solution)/shard_map/psum | solution.py:59
  506.1 13.1 %fusion.7 = f32[384,4096]{0,1:T(8,128)} fusion(bf16[768,384]{1,0:T(8,128)(2,1)S(1)} %copy-done, f32[4096,768]{0,1:T(8,128)} %get-tuple-element.18, f32[768,4096]{1,0:T(8,128)} %copy-done.1, f32[768]{0:T(1024)S(1)} %log.3, f32[768]{0:T(1024)S(1)} %get-tuple-element.12, f32[768]{0:T(1024)S(1)} %multiply_divide_fusion.3, f32[4096]{0:T(1024)S(1)} %multiply_divide_fusion), kind=kOutput, calls=%fused_computation.16 | convolution fusion | flops 2444230656 | bytes 32072704 | tf_op jit(solution)/shard_map/dot_general | solution.py:70
  519.2 6.5 copy.14
  525.8 15.7 %fusion = (f32[]{:T(128)}, bf16[768,4096]{1,0:T(8,128)(2,1)}) fusion(f32[4096,768]{0,1:T(8,128)} %get-tuple-element.18, f32[768]{0:T(1024)S(1)} %log.3, f32[768]{0:T(1024)S(1)} %get-tuple-element.12, f32[768]{0:T(1024)S(1)} %multiply_divide_fusion.3, f32[4096]{0:T(1024)S(1)} %multiply_divide_fusion, f32[768]{0:T(1024)S(1)} %get-tuple-element.11, ...), kind=kLoop, calls=%fused_computation.2 | loop fusion | flops 37748736 | bytes 31502340 | tf_op jit(solution)/shard_map/reduce_sum | solution.py:65
  543.4 80.6 %psum.70 = f32[]{:T(128)} all-reduce(f32[]{:T(128)S(6)} %neg.3), channel_id=1, replica_groups=mesh['dp'=8,'proto'=32] {'dp','proto'}, use_global_device_ids=true, to_apply=%region_15.16 | all-reduce | flops 1 | bytes 8 | tf_op jit(solution)/shard_map/psum | solution.py:67
  628.7 23.6 %psum.71 = f32[4096]{0:T(1024)S(1)} all-reduce(f32[4096]{0:T(1024)S(1)} %multiply_reduce_fusion.2), channel_id=1, replica_groups=mesh['dp'=8,'proto'=32] {'dp'}, use_global_device_ids=true, to_apply=%region_18.19 | all-reduce | flops 4096 | bytes 32768 | tf_op jit(solution)/shard_map/psum | solution.py:77
  652.3 4.6 subtract_divide_fusion
  656.9 3.1 copy.12
  (52 shorter events, 10.9 us)
Async XLA Ops:
  7.2 36.6 %copy-start = (bf16[768,384]{1,0:T(8,128)(2,1)S(1)}, bf16[768,384]{1,0:T(8,128)(2,1)}, u32[]{:S(2)}) copy-start(bf16[768,384]{1,0:T(8,128)(2,1)} %param.5) | copy-start | bytes 1769476
  7.2 35.4 %copy-start.2 = (bf16[48,4096]{1,0:T(8,128)(2,1)S(1)}, bf16[48,4096]{1,0:T(8,128)(2,1)}, u32[]{:S(2)}) copy-start(bf16[48,4096]{1,0:T(8,128)(2,1)} %param.7) | copy-start | bytes 1179652
  7.2 58.4 %all-gather.2.cloned.1.call-start = ((), (), s32[]{:S(2)}) async-start(), calls=%async_computation.1 | async-start | bytes 3538944 | tf_op jit(solution)/shard_map/all_gather | solution.py:34
  7.2 8.6 %collective-permute-start = (bf16[48,4096]{1,0:T(8,128)(2,1)}, bf16[48,4096]{1,0:T(8,128)(2,1)S(1)}, u32[]{:S(2)}, u32[]{:S(2)}) collective-permute-start(bf16[48,4096]{1,0:T(8,128)(2,1)} %param.7), channel_id=1, source_target_pairs={{0,32},{32,64},{64,96},{96,128},{128,160},{160,192},{192,224},{224... | collective-permute-start | bytes 1179656 | tf_op jit(solution)/shard_map/ppermute | solution.py:18
  15.9 8.4 %collective-permute-start.1 = (bf16[48,4096]{1,0:T(8,128)(2,1)S(1)}, bf16[48,4096]{1,0:T(8,128)(2,1)S(1)}, u32[]{:S(2)}, u32[]{:S(2)}) collective-permute-start(bf16[48,4096]{1,0:T(8,128)(2,1)S(1)} %collective-permute-done), channel_id=1, source_target_pairs={{0,32},{32,64},{64,96},{96,128},{128,160},{160,192},{192,224},{224... | collective-permute-start | bytes 1179656 | tf_op jit(solution)/shard_map/ppermute | solution.py:18
  15.9 8.6 %collective-permute-start.4 = (bf16[48,4096]{1,0:T(8,128)(2,1)}, bf16[48,4096]{1,0:T(8,128)(2,1)S(1)}, u32[]{:S(2)}, u32[]{:S(2)}) collective-permute-start(bf16[48,4096]{1,0:T(8,128)(2,1)} %param.7), channel_id=1, source_target_pairs={{0,224},{32,0},{64,32},{96,64},{128,96},{160,128},{192,160},{224,1... | collective-permute-start | bytes 1179656 | tf_op jit(solution)/shard_map/ppermute | solution.py:20
  24.3 8.4 %collective-permute-start.2 = (bf16[48,4096]{1,0:T(8,128)(2,1)S(1)}, bf16[48,4096]{1,0:T(8,128)(2,1)S(1)}, u32[]{:S(2)}, u32[]{:S(2)}) collective-permute-start(bf16[48,4096]{1,0:T(8,128)(2,1)S(1)} %collective-permute-done.1), channel_id=1, source_target_pairs={{0,32},{32,64},{64,96},{96,128},{128,160},{160,192},{192,224},{224... | collective-permute-start | bytes 1179656 | tf_op jit(solution)/shard_map/ppermute | solution.py:18
  24.4 8.4 %collective-permute-start.5 = (bf16[48,4096]{1,0:T(8,128)(2,1)S(1)}, bf16[48,4096]{1,0:T(8,128)(2,1)S(1)}, u32[]{:S(2)}, u32[]{:S(2)}) collective-permute-start(bf16[48,4096]{1,0:T(8,128)(2,1)S(1)} %collective-permute-done.4), channel_id=1, source_target_pairs={{0,224},{32,0},{64,32},{96,64},{128,96},{160,128},{192,160},{224,1... | collective-permute-start | bytes 1179656 | tf_op jit(solution)/shard_map/ppermute | solution.py:20
  32.7 8.4 %collective-permute-start.3 = (bf16[48,4096]{1,0:T(8,128)(2,1)S(1)}, bf16[48,4096]{1,0:T(8,128)(2,1)S(1)}, u32[]{:S(2)}, u32[]{:S(2)}) collective-permute-start(bf16[48,4096]{1,0:T(8,128)(2,1)S(1)} %collective-permute-done.2), channel_id=1, source_target_pairs={{0,32},{32,64},{64,96},{96,128},{128,160},{160,192},{192,224},{224... | collective-permute-start | bytes 1179656 | tf_op jit(solution)/shard_map/ppermute | solution.py:18
  32.7 591.9 %reduce-scatter.4.cloned.1.call-start = ((), (), s32[]{:S(2)}) async-start(), calls=%async_computation.2 | async-start | bytes 7077888
  32.8 9.5 %collective-permute-start.6 = (bf16[48,4096]{1,0:T(8,128)(2,1)S(1)}, bf16[48,4096]{1,0:T(8,128)(2,1)S(1)}, u32[]{:S(2)}, u32[]{:S(2)}) collective-permute-start(bf16[48,4096]{1,0:T(8,128)(2,1)S(1)} %collective-permute-done.5), channel_id=1, source_target_pairs={{0,224},{32,0},{64,32},{96,64},{128,96},{160,128},{192,160},{224,1... | collective-permute-start | bytes 1179656 | tf_op jit(solution)/shard_map/ppermute | solution.py:20
  43.8 24.4 %copy-start.3 = (bf16[768,384]{1,0:T(8,128)(2,1)S(1)}, bf16[768,384]{1,0:T(8,128)(2,1)}, u32[]{:S(2)}) copy-start(bf16[768,384]{1,0:T(8,128)(2,1)} %param.4) | copy-start | bytes 1769476
  153.1 6.0 copy-start.1
Sparse Core Ops, SparseCore 0:
  32.8 32.7 all-gather.1
  525.9 46.9 reduce-scatter.3
